TPU v7x, 256 devices: a whole 4x4x8 slice. The times are simulated.
256 devices in a mesh: cam: 8 (over x, core), clip: 32 (over y, z).
Axes of the slice: x: 4, y: 4, z: 8, core: 2. Of those that a mesh axis runs over, the one named last changes fastest.
Arguments:
- tokens: bfloat16 [64, 8, 256, 1024], P('clip', 'cam'), may hold values from -6 to 6
- w_query: bfloat16 [1024, 1024], replicated, may hold values from -0.1875 to 0.1875
- w_key: bfloat16 [1024, 1024], replicated, may hold values from -0.1875 to 0.1875
- w_value: bfloat16 [1024, 1024], replicated, may hold values from -0.1875 to 0.1875
- w_proj: bfloat16 [1024, 256], replicated, may hold values from -0.1875 to 0.1875
- prototypes: bfloat16 [256, 65536], P(None, ('cam', 'clip')), may hold values from -6 to 6
Outputs:
- codes: float32 [64, 65536], P(None, ('cam', 'clip'))
- prototype_gradient: float32 [256, 65536], P(None, ('cam', 'clip'))
- grad_proj: float32 [1024, 256], P('clip')
- grad_value: float32 [1024, 1024], P('clip', 'cam')
All inputs are finite; a program needn't handle non-finite values.
Results may differ from a plain program's by a relative error of at most 0.015.
Values may be sent and summed in bfloat16 or wider, within the bound.
A program may use at most 128 MiB of HBM per device.

v0:
```python
import jax
import jax.numpy as jnp
from jax import lax
from jax.sharding import PartitionSpec as P

D = 1024
HD = 64
PROTOS = 65536
TOK = 256
ITERS = 3
H = 16
SINK_EPS = 0.05
SOFTMAX_TEMP = 0.1
NORM_EPS = 1e-06
heads_per_group = 4


def column_sums(query_rows, key_rows, total):
    scores = jnp.einsum(
        "ihe,jhe->hij", query_rows, key_rows, preferred_element_type=jnp.float32
    ) * HD ** (-0.5)
    exponent_values = jnp.exp(scores)
    probs = exponent_values / jnp.sum(exponent_values, axis=2, keepdims=True)
    return jnp.sum(probs, axis=1) / total


def camera_block(query_clip, key_clip, total):
    tokens_here = query_clip.shape[0]
    width = heads_per_group * HD
    parts = []
    for group in range(H // heads_per_group):
        query_group = query_clip[:, group * width : (group + 1) * width].reshape(
            tokens_here, heads_per_group, HD
        )
        key_group = key_clip[:, group * width : (group + 1) * width].reshape(
            total, heads_per_group, HD
        )
        parts.append(column_sums(query_group, key_group, total))
    return jnp.concatenate(parts, axis=0)


def local(tokens, w_query, w_key, w_value, w_proj, prototypes):
    clips = tokens.shape[0]
    own = tokens.reshape(clips, TOK, D)
    query_vectors = jnp.einsum(
        "ctd,de->cte", own, w_query, preferred_element_type=jnp.float32
    ).astype(jnp.bfloat16)
    key_rows = jnp.einsum("ctd,de->cte", own, w_key, preferred_element_type=jnp.float32).astype(
        jnp.bfloat16
    )
    collected_rows = lax.all_gather(key_rows.reshape(clips, 1, TOK, D), "cam", axis=1, tiled=True)
    cameras = collected_rows.shape[1]
    total = cameras * TOK

    def per_clip(clip_pair):
        return camera_block(clip_pair[0], clip_pair[1], total)

    partial_sums = lax.map(per_clip, (query_vectors, collected_rows.reshape(clips, total, D)))
    weights = lax.psum_scatter(
        partial_sums.reshape(clips, H, cameras, TOK), "cam", scatter_dimension=2, tiled=True
    )
    weights = weights.reshape(clips, H, TOK).astype(jnp.bfloat16)
    mixture = jnp.einsum("chj,cjd->chd", weights, own, preferred_element_type=jnp.float32).astype(
        jnp.bfloat16
    )
    head_out = jnp.einsum(
        "chd,dhe->che", mixture, w_value.reshape(D, H, HD), preferred_element_type=jnp.float32
    )
    pooled = lax.psum(head_out.reshape(clips, D), "cam").astype(jnp.bfloat16)
    share_rows = D // lax.axis_size("clip")
    embed = jnp.dot(pooled, w_proj, preferred_element_type=jnp.float32)
    embed_norm = jnp.sqrt(jnp.sum(embed * embed, axis=1, keepdims=True) + NORM_EPS)
    unit = embed / embed_norm
    unit_b = unit.astype(jnp.bfloat16)
    all_units = lax.all_gather(unit_b, "clip", axis=0, tiled=True)
    proto_f = prototypes.astype(jnp.float32)
    column_norm = jnp.sqrt(jnp.sum(proto_f * proto_f, axis=0, keepdims=True) + NORM_EPS)
    unit_proto = proto_f / column_norm
    proto_b = unit_proto.astype(jnp.bfloat16)
    logit_scores = jnp.dot(all_units, proto_b, preferred_element_type=jnp.float32)
    exponent_values = jnp.exp(logit_scores / SOFTMAX_TEMP)
    assign = jnp.exp(logit_scores / SINK_EPS)
    prob_total = lax.psum(jnp.sum(exponent_values, axis=1), ("cam", "clip"))
    first_step = 0
    for step in range(first_step, ITERS):
        assign = assign / jnp.sum(assign, axis=0, keepdims=True)
        row_total = lax.psum(jnp.sum(assign, axis=1), ("cam", "clip"))
        assign = assign / row_total[:, None]
    prob = exponent_values / prob_total[:, None]
    grad_logits = (PROTOS * (prob - assign)).astype(jnp.bfloat16)
    codes = PROTOS * assign
    grad_unit = lax.psum_scatter(
        jnp.dot(grad_logits, proto_b.T, preferred_element_type=jnp.float32),
        "clip",
        scatter_dimension=0,
        tiled=True,
    )
    grad_unit = lax.psum(grad_unit, "cam")
    grad_embed = (grad_unit - unit * jnp.sum(unit * grad_unit, axis=1, keepdims=True)) / embed_norm
    grad_embed_b = grad_embed.astype(jnp.bfloat16)
    grad_pooled = jnp.dot(grad_embed_b, w_proj.T, preferred_element_type=jnp.float32).astype(
        jnp.bfloat16
    )
    piece = pooled
    grad_proj = lax.psum_scatter(
        jnp.einsum("cd,ce->de", piece, grad_embed_b, preferred_element_type=jnp.float32),
        "clip",
        scatter_dimension=0,
        tiled=True,
    )
    grad_heads = grad_pooled.reshape(clips, H, HD)
    piece = lax.slice_in_dim(mixture, 0, share_rows * lax.axis_size("clip"), axis=2)
    value_rows = lax.psum_scatter(
        jnp.einsum("chd,che->dhe", piece, grad_heads, preferred_element_type=jnp.float32).reshape(
            share_rows * lax.axis_size("clip"), D
        ),
        "clip",
        scatter_dimension=0,
        tiled=True,
    )
    grad_value = lax.psum_scatter(value_rows, "cam", scatter_dimension=1, tiled=True)
    grad_unit_proto = jnp.einsum(
        "be,bk->ek", all_units, grad_logits, preferred_element_type=jnp.float32
    )
    prototype_gradient = (
        grad_unit_proto - unit_proto * jnp.sum(unit_proto * grad_unit_proto, axis=0, keepdims=True)
    ) / column_norm
    return (codes, prototype_gradient, grad_proj, grad_value)


def solution(mesh):
    in_specs = (P("clip", "cam", None, None), P(), P(), P(), P(), P(None, ("cam", "clip")))
    out_specs = (
        P(None, ("cam", "clip")),
        P(None, ("cam", "clip")),
        P("clip", None),
        P("clip", "cam"),
    )
    return jax.shard_map(local, mesh=mesh, in_specs=in_specs, out_specs=out_specs, check_vma=False)
```

profile of v0, /device:TPU:8, one launch (start us, length us, event | category | flops | bytes accessed | tf_op | source)
XLA Modules:
  0.0 1159.4 jit_solution(2229369669846176685)
XLA Ops:
  20.2 47.3 %all-gather.4.cloned.1.call-done = bf16[2,2048,1024]{2,1,0:T(8,128)(2,1)} async-done(((bf16[2,256,1024]{2,1,0:T(8,128)(2,1)}), bf16[2,2048,1024]{2,1,0:T(8,128)(2,1)}) %all-gather.4.cloned.1.call-update) | async-done | bytes 8388624 | tf_op jit(solution)/shard_map/all_gather | solution.py:51
  67.5 130.2 %while.10 = (s32[]{:T(128)}, f32[2,16,2048]{2,1,0:T(8,128)}, bf16[2,256,1024]{2,1,0:T(8,128)(2,1)}, bf16[2,2048,1024]{2,1,0:T(8,128)(2,1)}, s32[]{:T(128)}) while((s32[]{:T(128)}, f32[2,16,2048]{2,1,0:T(8,128)}, bf16[2,256,1024]{2,1,0:T(8,128)(2,1)}, bf16[2,2048,1024]{2,1,0:T(8,128)(2,1)}, s32[]{:T(128)}) %tuple.47), condition=%wide.region_9.10_spmd, body=%wide.region_0.9_spmd.sunk | while | flops 2181148672 | bytes 112328888 | solution.py:58
  67.5 4.6 constant_dynamic-slice_fusion.6
  72.1 6.5 copy.50
  87.1 5.7 fusion.143
  92.9 7.5 divide_reduce_fusion.11
  104.8 6.1 divide_reduce_fusion.12
  111.8 4.5 fusion.142
  116.3 5.5 divide_reduce_fusion.10
  121.8 4.5 fusion.141
  126.3 5.6 divide_reduce_fusion.9
  132.7 4.6 constant_dynamic-slice_fusion.6
  137.3 6.5 copy.50
  152.3 5.7 fusion.143
  158.0 7.5 divide_reduce_fusion.11
  169.9 6.1 divide_reduce_fusion.12
  176.9 4.5 fusion.142
  181.4 5.5 divide_reduce_fusion.10
  186.9 4.5 fusion.141
  191.4 5.6 divide_reduce_fusion.9
  201.4 31.9 %reduce-scatter.5.cloned.1.call-done = f32[2,16,1,256]{3,1,0,2:T(8,128)} async-done(((f32[2,16,8,256]{3,1,0,2:T(8,128)}), f32[2,16,1,256]{3,1,0,2:T(8,128)}) %reduce-scatter.5.cloned.1.call-update) | async-done | bytes 32784 | tf_op jit(solution)/shard_map/reduce_scatter | solution.py:59
  237.1 13.2 %psum.42 = bf16[2,1024]{1,0:T(2,128)(2,1)S(1)} all-reduce(f32[2,1024]{1,0:T(2,128)S(1)} %reshape.88), channel_id=1, replica_groups=mesh['cam'=8,'clip'=32] {'cam'}, use_global_device_ids=true, to_apply=%region_11.12 | all-reduce | flops 2048 | bytes 12288 | tf_op jit(solution)/shard_map/psum | solution.py:69
  251.7 43.0 %all-gather.1 = bf16[32,2,256]{2,1,0:T(2,128)(2,1)S(1)} all-gather(bf16[1,2,256]{2,1,0:T(2,128)(2,1)S(1)} %get-tuple-element.51), channel_id=1, replica_groups=mesh['cam'=8,'clip'=32] {'clip'}, dimensions={0}, use_global_device_ids=true | all-gather | bytes 33792 | tf_op jit(solution)/shard_map/all_gather | solution.py:75
  295.1 72.7 %psum.43 = f32[64]{0:T(128)S(1)} all-reduce(f32[64]{0:T(128)S(1)} %get-tuple-element.40), channel_id=1, replica_groups=mesh['cam'=8,'clip'=32] {'cam','clip'}, use_global_device_ids=true, to_apply=%region_16.17 | all-reduce | flops 64 | bytes 512 | tf_op jit(solution)/shard_map/psum | solution.py:87
  368.0 74.3 %psum.44 = f32[64]{0:T(128)S(1)} all-reduce(f32[64]{0:T(128)S(1)} %fusion.48), channel_id=1, replica_groups=mesh['cam'=8,'clip'=32] {'cam','clip'}, use_global_device_ids=true, to_apply=%region_19.20 | all-reduce | flops 64 | bytes 512 | tf_op jit(solution)/shard_map/psum | solution.py:87
  442.6 73.4 %all-reduce.1 = (f32[64]{0:T(128)S(1)}, f32[64]{0:T(128)S(1)}) all-reduce(f32[64]{0:T(128)S(1)} %fusion.50, f32[64]{0:T(128)S(1)} %get-tuple-element.39), channel_id=1, replica_groups=mesh['cam'=8,'clip'=32] {'cam','clip'}, use_global_device_ids=true, to_apply=%region_22.23 | all-reduce | flops 128 | bytes 1024 | tf_op jit(solution)/shard_map/psum | solution.py:87
  518.8 137.5 %all-reduce.4.cloned.1.call-done = f32[64,256]{1,0:T(8,128)} async-done(((f32[64,256]{1,0:T(8,128)}), f32[64,256]{1,0:T(8,128)}) %all-reduce.4.cloned.1.call-update) | async-done | bytes 65552
  657.1 12.4 %psum.47 = f32[2,256]{1,0:T(2,128)S(1)} all-reduce(f32[2,256]{1,0:T(2,128)S(1)} %constant_dynamic-slice_fusion.2), channel_id=1, replica_groups=mesh['cam'=8,'clip'=32] {'cam'}, use_global_device_ids=true, to_apply=%region_27.28 | all-reduce | flops 512 | bytes 4096 | tf_op jit(solution)/shard_map/psum | solution.py:98
  673.7 5.4 copy.35
  680.6 217.1 %reduce-scatter.9.cloned.1.call-done = f32[32,1024]{1,0:T(8,128)} async-done(((f32[1024,1024]{1,0:T(8,128)}), f32[32,1024]{1,0:T(8,128)}) %reduce-scatter.9.cloned.1.call-update) | async-done | bytes 131088 | tf_op jit(solution)/shard_map/reduce_scatter | solution.py:113
  898.7 218.6 %reduce-scatter.7.cloned.1.call-done = f32[32,256]{1,0:T(8,128)} async-done(((f32[1024,256]{1,0:T(8,128)}), f32[32,256]{1,0:T(8,128)}) %reduce-scatter.7.cloned.1.call-update) | async-done | bytes 32784 | tf_op jit(solution)/shard_map/reduce_scatter | solution.py:105
  1117.3 35.2 %reduce-scatter.11.cloned.1.call-done = f32[32,128]{1,0:T(8,128)} async-done(((f32[32,1024]{1,0:T(8,128)}), f32[32,128]{1,0:T(8,128)}) %reduce-scatter.11.cloned.1.call-update) | async-done | bytes 16400 | tf_op jit(solution)/shard_map/reduce_scatter | solution.py:121
  (87 shorter events, 61.5 us)
Async XLA Ops:
  7.2 1.6 copy-start
  7.2 9.2 copy-start.5
  7.2 60.4 %all-gather.4.cloned.1.call-start = ((), (), s32[]{:S(2)}) async-start(), calls=%async_computation.8 | async-start | bytes 9437184 | tf_op jit(solution)/shard_map/all_gather | solution.py:51
  12.3 221.0 %reduce-scatter.5.cloned.1.call-start = ((), (), s32[]{:S(2)}) async-start(), calls=%async_computation.4 | async-start | bytes 294912 | tf_op jit(solution)/shard_map/reduce_scatter | solution.py:59
  67.5 450.1 %copy-start.8 = (u32[256]{0:T(256)S(1)}, u32[256]{0:T(256)}, u32[]{:S(2)}) copy-start(u32[256]{0:T(256)} %constant.40) | copy-start | bytes 3076
  78.6 3.8 copy-start.3
  86.5 0.6 copy-start.2
  126.3 5.6 copy-start.6
  132.0 0.7 copy-start.7
  143.7 3.8 copy-start.3
  151.6 0.6 copy-start.2
  191.4 5.6 copy-start.6
  197.1 0.7 copy-start.7
  199.5 456.9 %all-reduce.4.cloned.1.call-start = ((), (), s32[]{:S(2)}) async-start(), calls=%async_computation.9 | async-start | bytes 131072
  517.5 380.1 %reduce-scatter.9.cloned.1.call-start = ((), (), s32[]{:S(2)}) async-start(), calls=%async_computation.6 | async-start | bytes 4325376 | tf_op jit(solution)/shard_map/reduce_scatter | solution.py:113
  671.0 481.5 %copy-start.1 = (bf16[1024,1024]{1,0:T(8,128)(2,1)S(1)}, bf16[1024,1024]{1,0:T(8,128)(2,1)}, u32[]{:S(2)}) copy-start(bf16[1024,1024]{1,0:T(8,128)(2,1)} %param.10) | copy-start | bytes 6291460
  673.7 224.0 %copy-start.4 = (bf16[256,256]{1,0:T(8,128)(2,1)S(1)}, bf16[256,256]{1,0:T(8,128)(2,1)}, u32[]{:S(2)}) copy-start(bf16[256,256]{1,0:T(8,128)(2,1)} %param.13) | copy-start | bytes 393220
  679.1 438.2 %reduce-scatter.7.cloned.1.call-start = ((), (), s32[]{:S(2)}) async-start(), calls=%async_computation.5 | async-start | bytes 1081344 | tf_op jit(solution)/shard_map/reduce_scatter | solution.py:105
  680.5 472.0 %reduce-scatter.11.cloned.1.call-start = ((), (), s32[]{:S(2)}) async-start(), calls=%async_computation.7 | async-start | bytes 147456 | tf_op jit(solution)/shard_map/reduce_scatter | solution.py:121
Sparse Core Ops, SparseCore 0:
  12.5 55.0 all-gather.3
  199.6 33.6 reduce-scatter.4
  517.7 138.6 all-reduce.3
  679.3 218.3 reduce-scatter.8
  901.9 215.3 reduce-scatter.6
  1120.2 32.2 reduce-scatter.10
where the time goes:
time: 1160 us
  waiting for transfers between devices  688 us (59%)
  blocking collectives  289 us (25%)
  matrix products  107 us (9%)
  local copies, waits for them, and re-layouts  54.6 us (5%)
  between operations  14.9 us (1%)
    psum x3, blocking collectives, local(): row_total = lax.psum(jnp.sum(assign, axis=1), ('cam', 'clip'))  220 us
    reduce_scatter x1, waiting for transfers between devices, local(): lax.psum_scatter(jnp.einsum('cd,ce->de', piece, grad_embed_b, preferred_e...  219 us
    reduce_scatter x1, waiting for transfers between devices, local(): lax.psum_scatter(jnp.einsum('chd,che->dhe', piece, grad_heads, preferred_...  217 us
    unnamed x7, waiting for transfers between devices  138 us
    div x8, matrix products, column_sums(): probs = exponent_values / jnp.sum(exponent_values, axis=2, keepdims=True)  49.5 us
    all_gather x1, waiting for transfers between devices, local(): lax.all_gather(key_rows.reshape(clips, 1, TOK, D), 'cam', axis=1, tiled=T...  47.3 us
    all_gather x1, blocking collectives, local(): all_units = lax.all_gather(unit_b, 'clip', axis=0, tiled=True)  43 us
    dot_general x8, matrix products, column_sums(): jnp.einsum('ihe,jhe->hij', query_rows, key_rows, preferred_element_type=j...  38.4 us
  transfers between devices with their start and end apart: 6, of which 6 were waited for; matrix products, arithmetic and copies ran while one was open for 1% of the time, Pallas kernels for 0%

commit v1 on v0

--- a/solution.py
+++ b/solution.py
@@ -84,7 +84,7 @@
     first_step = 0
     for step in range(first_step, ITERS):
         assign = assign / jnp.sum(assign, axis=0, keepdims=True)
-        row_total = lax.psum(jnp.sum(assign, axis=1), ("cam", "clip"))
+        row_total = jnp.sum(lax.all_gather(jnp.sum(assign, axis=1), ("cam", "clip")), axis=0)
         assign = assign / row_total[:, None]
     prob = exponent_values / prob_total[:, None]
     grad_logits = (PROTOS * (prob - assign)).astype(jnp.bfloat16)

time: 1160 us -> 1670 us (1.44)
  waiting for transfers between devices: 688 us -> 1340 us
  blocking collectives: 289 us -> 143 us
    unnamed x7 -> x13, waiting for transfers between devices: 138 us -> 786 us
    psum x3 -> x1, blocking collectives: 220 us -> 74.3 us  [local(): prob_total = lax.psum(jnp.sum(exponent_values, axis=1), ('cam', 'clip'))]
  transfers between devices with their start and end apart: 6 -> 9, of which waited for: 6 -> 9; matrix products, arithmetic and copies ran while one was open for 1% -> 1% of each run, Pallas kernels for 0% -> 0%
where the time goes in v1:
time: 1670 us
  waiting for transfers between devices  1340 us (80%)
  blocking collectives  143 us (9%)
  matrix products  107 us (6%)
  local copies, waits for them, and re-layouts  60.1 us (4%)
    unnamed x13, waiting for transfers between devices  786 us
    reduce_scatter x1, waiting for transfers between devices, local(): lax.psum_scatter(jnp.einsum('cd,ce->de', piece, grad_embed_b, preferred_e...  219 us
    reduce_scatter x1, waiting for transfers between devices, local(): lax.psum_scatter(jnp.einsum('chd,che->dhe', piece, grad_heads, preferred_...  217 us
    psum x1, blocking collectives, local(): prob_total = lax.psum(jnp.sum(exponent_values, axis=1), ('cam', 'clip'))  74.3 us
    div x8, matrix products, column_sums(): probs = exponent_values / jnp.sum(exponent_values, axis=2, keepdims=True)  49.5 us
    all_gather x1, waiting for transfers between devices, local(): lax.all_gather(key_rows.reshape(clips, 1, TOK, D), 'cam', axis=1, tiled=T...  47.3 us
    all_gather x1, blocking collectives, local(): all_units = lax.all_gather(unit_b, 'clip', axis=0, tiled=True)  43 us
    dot_general x8, matrix products, column_sums(): jnp.einsum('ihe,jhe->hij', query_rows, key_rows, preferred_element_type=j...  38.4 us
  transfers between devices with their start and end apart: 9, of which 9 were waited for; matrix products, arithmetic and copies ran while one was open for 1% of the time, Pallas kernels for 0%

profile of v1, /device:TPU:8, one launch (start us, length us, event | category | flops | bytes accessed | tf_op | source)
XLA Modules:
  0.0 1667.2 jit_solution(16680891827759426276)
XLA Ops:
  20.2 47.3 %all-gather.7.cloned.1.call-done = bf16[2,2048,1024]{2,1,0:T(8,128)(2,1)} async-done(((bf16[2,256,1024]{2,1,0:T(8,128)(2,1)}), bf16[2,2048,1024]{2,1,0:T(8,128)(2,1)}) %all-gather.7.cloned.1.call-update) | async-done | bytes 8388624 | tf_op jit(solution)/shard_map/all_gather | solution.py:51
  67.5 130.2 %while.10 = (s32[]{:T(128)}, f32[2,16,2048]{2,1,0:T(8,128)}, bf16[2,256,1024]{2,1,0:T(8,128)(2,1)}, bf16[2,2048,1024]{2,1,0:T(8,128)(2,1)}, s32[]{:T(128)}) while((s32[]{:T(128)}, f32[2,16,2048]{2,1,0:T(8,128)}, bf16[2,256,1024]{2,1,0:T(8,128)(2,1)}, bf16[2,2048,1024]{2,1,0:T(8,128)(2,1)}, s32[]{:T(128)}) %tuple.47), condition=%wide.region_9.10_spmd, body=%wide.region_0.9_spmd.sunk | while | flops 2181148672 | bytes 112328888 | solution.py:58
  67.5 4.6 constant_dynamic-slice_fusion.6
  72.1 6.5 copy.50
  87.1 5.7 fusion.143
  92.9 7.5 divide_reduce_fusion.11
  104.8 6.1 divide_reduce_fusion.12
  111.8 4.5 fusion.142
  116.3 5.5 divide_reduce_fusion.10
  121.8 4.5 fusion.141
  126.3 5.6 divide_reduce_fusion.9
  132.7 4.6 constant_dynamic-slice_fusion.6
  137.3 6.5 copy.50
  152.3 5.7 fusion.143
  158.0 7.5 divide_reduce_fusion.11
  169.9 6.1 divide_reduce_fusion.12
  176.9 4.5 fusion.142
  181.4 5.5 divide_reduce_fusion.10
  191.4 5.6 divide_reduce_fusion.9
  201.4 31.9 %reduce-scatter.5.cloned.1.call-done = f32[2,16,1,256]{3,1,0,2:T(8,128)} async-done(((f32[2,16,8,256]{3,1,0,2:T(8,128)}), f32[2,16,1,256]{3,1,0,2:T(8,128)}) %reduce-scatter.5.cloned.1.call-update) | async-done | bytes 32784 | tf_op jit(solution)/shard_map/reduce_scatter | solution.py:59
  237.1 13.2 psum.21
  251.7 43.0 %all-gather.4 = bf16[32,2,256]{2,1,0:T(2,128)(2,1)S(1)} all-gather(bf16[1,2,256]{2,1,0:T(2,128)(2,1)S(1)} %get-tuple-element.49), channel_id=1, replica_groups=mesh['cam'=8,'clip'=32] {'clip'}, dimensions={0}, use_global_device_ids=true | all-gather | bytes 33792 | tf_op jit(solution)/shard_map/all_gather | solution.py:75
  296.1 237.6 %all-reduce.9.cloned.1.call-done = f32[16384]{0:T(1024)} async-done(((f32[16384]{0:T(1024)}), f32[16384]{0:T(1024)}) %all-reduce.9.cloned.1.call-update) | async-done | bytes 65552
  535.9 241.6 %all-reduce.11.cloned.1.call-done = f32[16384]{0:T(1024)} async-done(((f32[16384]{0:T(1024)}), f32[16384]{0:T(1024)}) %all-reduce.11.cloned.1.call-update) | async-done | bytes 65552
  779.7 74.3 %psum.22 = f32[64]{0:T(128)S(1)} all-reduce(f32[64]{0:T(128)S(1)} %get-tuple-element.39), channel_id=1, replica_groups=mesh['cam'=8,'clip'=32] {'cam','clip'}, use_global_device_ids=true, to_apply=%region_24.25 | all-reduce | flops 64 | bytes 512 | tf_op jit(solution)/shard_map/psum | solution.py:83
  854.0 167.7 %all-reduce.13.cloned.1.call-done = f32[16384]{0:T(1024)} async-done(((f32[16384]{0:T(1024)}), f32[16384]{0:T(1024)}) %all-reduce.13.cloned.1.call-update) | async-done | bytes 65552
  1025.5 138.8 %all-reduce.15.cloned.1.call-done = f32[64,256]{1,0:T(8,128)} async-done(((f32[64,256]{1,0:T(8,128)}), f32[64,256]{1,0:T(8,128)}) %all-reduce.15.cloned.1.call-update) | async-done | bytes 65552
  1165.0 12.4 psum.23
  1181.6 5.4 copy.35
  1188.5 216.9 %reduce-scatter.9.cloned.1.call-done = f32[32,1024]{1,0:T(8,128)} async-done(((f32[1024,1024]{1,0:T(8,128)}), f32[32,1024]{1,0:T(8,128)}) %reduce-scatter.9.cloned.1.call-update) | async-done | bytes 131088 | tf_op jit(solution)/shard_map/reduce_scatter | solution.py:113
  1406.5 218.7 %reduce-scatter.7.cloned.1.call-done = f32[32,256]{1,0:T(8,128)} async-done(((f32[1024,256]{1,0:T(8,128)}), f32[32,256]{1,0:T(8,128)}) %reduce-scatter.7.cloned.1.call-update) | async-done | bytes 32784 | tf_op jit(solution)/shard_map/reduce_scatter | solution.py:105
  1625.1 35.5 %reduce-scatter.11.cloned.1.call-done = f32[32,128]{1,0:T(8,128)} async-done(((f32[32,1024]{1,0:T(8,128)}), f32[32,128]{1,0:T(8,128)}) %reduce-scatter.11.cloned.1.call-update) | async-done | bytes 16400 | tf_op jit(solution)/shard_map/reduce_scatter | solution.py:121
  (112 shorter events, 71.8 us)
Async XLA Ops:
  7.2 1.6 copy-start
  7.2 9.2 copy-start.5
  7.2 60.4 %all-gather.7.cloned.1.call-start = ((), (), s32[]{:S(2)}) async-start(), calls=%async_computation.8 | async-start | bytes 9437184 | tf_op jit(solution)/shard_map/all_gather | solution.py:51
  12.3 221.0 %reduce-scatter.5.cloned.1.call-start = ((), (), s32[]{:S(2)}) async-start(), calls=%async_computation.4 | async-start | bytes 294912 | tf_op jit(solution)/shard_map/reduce_scatter | solution.py:59
  67.5 956.7 %copy-start.11 = (u32[256]{0:T(256)S(1)}, u32[256]{0:T(256)}, u32[]{:S(2)}) copy-start(u32[256]{0:T(256)} %constant.52) | copy-start | bytes 3076
  78.6 3.8 copy-start.3
  86.5 0.6 copy-start.2
  126.3 5.6 copy-start.6
  132.0 0.7 copy-start.7
  143.7 3.8 copy-start.3
  151.6 0.6 copy-start.2
  191.4 5.6 copy-start.6
  197.1 0.7 copy-start.7
  199.5 334.1 %all-reduce.9.cloned.1.call-start = ((), (), s32[]{:S(2)}) async-start(), calls=%async_computation.9 | async-start | bytes 131072
  295.4 0.6 copy-start.9
  296.0 481.5 %all-reduce.11.cloned.1.call-start = ((), (), s32[]{:S(2)}) async-start(), calls=%async_computation.10 | async-start | bytes 131072
  535.2 0.6 copy-start.10
  535.8 485.8 %all-reduce.13.cloned.1.call-start = ((), (), s32[]{:S(2)}) async-start(), calls=%async_computation.11 | async-start | bytes 131072
  779.0 0.6 copy-start.8
  779.7 384.6 %all-reduce.15.cloned.1.call-start = ((), (), s32[]{:S(2)}) async-start(), calls=%async_computation.12 | async-start | bytes 131072
  1024.2 381.2 %reduce-scatter.9.cloned.1.call-start = ((), (), s32[]{:S(2)}) async-start(), calls=%async_computation.6 | async-start | bytes 4325376 | tf_op jit(solution)/shard_map/reduce_scatter | solution.py:113
  1178.9 481.8 %copy-start.1 = (bf16[1024,1024]{1,0:T(8,128)(2,1)S(1)}, bf16[1024,1024]{1,0:T(8,128)(2,1)}, u32[]{:S(2)}) copy-start(bf16[1024,1024]{1,0:T(8,128)(2,1)} %param.10) | copy-start | bytes 6291460
  1181.6 223.8 %copy-start.4 = (bf16[256,256]{1,0:T(8,128)(2,1)S(1)}, bf16[256,256]{1,0:T(8,128)(2,1)}, u32[]{:S(2)}) copy-start(bf16[256,256]{1,0:T(8,128)(2,1)} %param.13) | copy-start | bytes 393220
  1187.1 438.1 %reduce-scatter.7.cloned.1.call-start = ((), (), s32[]{:S(2)}) async-start(), calls=%async_computation.5 | async-start | bytes 1081344 | tf_op jit(solution)/shard_map/reduce_scatter | solution.py:105
  1188.5 472.2 %reduce-scatter.11.cloned.1.call-start = ((), (), s32[]{:S(2)}) async-start(), calls=%async_computation.7 | async-start | bytes 147456 | tf_op jit(solution)/shard_map/reduce_scatter | solution.py:121
Sparse Core Ops, SparseCore 0:
  12.5 55.0 all-gather.6
  199.6 33.6 reduce-scatter.4
  296.1 237.4 all-reduce.8
  539.6 237.8 all-reduce.10
  783.4 238.2 all-reduce.12
  1025.6 138.6 all-reduce.14
  1187.2 218.2 reduce-scatter.8
  1409.8 215.2 reduce-scatter.6
  1628.2 32.4 reduce-scatter.10
